TPU v7x, 128 devices: a whole 4x4x4 slice. The times are simulated.
128 devices in a mesh: leaf: 16 (over z, y), front: 8 (over x, core).
Axes of the slice: x: 4, y: 4, z: 4, core: 2. Of those that a mesh axis runs over, the one named last changes fastest.
Arguments:
- right_side: bfloat16 [32, 81920], P(None, ('leaf', 'front')), may hold values from -6 to 6
- send_order: int32 [81920], P(('leaf', 'front')), may hold values from 0 to 639, as said below
- owner_order: int32 [81920], P(('leaf', 'front')), may hold values from 0 to 639, as said below
- live_rows: int32 [14], replicated, may hold values from 2048 to 4096, as said below
- lower_leaf: bfloat16 [1536, 24576], P(None, ('leaf', 'front')), may hold values from -0.109375 to 0.109375
- upper_leaf: bfloat16 [1536, 24576], P(None, ('leaf', 'front')), may hold values from -0.109375 to 0.109375
- lower_first: bfloat16 [4096, 32768], P(None, ('leaf', 'front')), may hold values from -0.0625 to 0.0625
- lower_second: bfloat16 [4096, 16384], P(None, ('leaf', 'front')), may hold values from -0.0625 to 0.0625
- lower_third: bfloat16 [4096, 8192], P(None, ('leaf', 'front')), may hold values from -0.0625 to 0.0625
- upper_first: bfloat16 [4096, 32768], P(None, ('leaf', 'front')), may hold values from -0.0625 to 0.0625
- upper_second: bfloat16 [4096, 16384], P(None, ('leaf', 'front')), may hold values from -0.0625 to 0.0625
- upper_third: bfloat16 [4096, 8192], P(None, ('leaf', 'front')), may hold values from -0.0625 to 0.0625
- downlink_first: bfloat16 [4096, 24576], P(None, ('leaf', 'front')), may hold values from -0.4375 to 0.4375
- downlink_second: bfloat16 [4096, 32768], P(None, ('leaf', 'front')), may hold values from -0.25 to 0.25
- downlink_third: bfloat16 [4096, 16384], P(None, ('leaf', 'front')), may hold values from -0.25 to 0.25
- uplink_first: bfloat16 [4096, 24576], P(None, ('leaf', 'front')), may hold values from -0.0625 to 0.0625
- uplink_second: bfloat16 [4096, 32768], P(None, ('leaf', 'front')), may hold values from -0.0625 to 0.0625
- uplink_third: bfloat16 [4096, 16384], P(None, ('leaf', 'front')), may hold values from -0.0625 to 0.0625
- pattern_first: int32 [64, 384], P(None, ('leaf', 'front')), may hold values 0 or 1
- pattern_second: int32 [64, 512], P(None, ('leaf', 'front')), may hold values 0 or 1
- pattern_third: int32 [64, 256], P(None, ('leaf', 'front')), may hold values 0 or 1
Outputs:
- solution: bfloat16 [32, 81920], P(None, ('leaf', 'front'))
Inputs may be any that keep to these rules, and one draw needn't show every extreme that they name: `send_order`: each device's 640 entries are a permutation of 0 to 639. `owner_order`: each device's 640 entries are a permutation of 0 to 639. `live_rows`: multiples of 64.
All inputs are finite; a program needn't handle non-finite values. No bound on the sum of `pattern_first` or of `pattern_second` or of `pattern_third` on one device may be relied on, other than what follows from the above.
Results may differ from a plain program's by a relative error of at most 0.023.
Values may be sent and summed in bfloat16 or wider, within the bound.
No kernel may reach another device: no remote copies, remote signals or barrier semaphores. Data moves between devices by JAX's collectives and lax.ppermute only.
A program may use at most 128 MiB of HBM per device.

v0:
```python
import jax
import jax.numpy as jnp
from jax import lax
from jax.sharding import PartitionSpec as P


def partner_2(value, axis, distance):
    mask = 2**distance
    pairs = [(source, source ^ mask) for source in range(lax.axis_size(axis))]
    return lax.ppermute(value, axis, pairs)


def spread(pattern, block):
    wide = jnp.repeat(pattern, block, axis=0)
    return jnp.repeat(wide, block, axis=1).astype(jnp.bfloat16)


def collect_group(portion, level, place):
    gathered = lax.all_gather(portion, "front", axis=1, tiled=True)
    for level_bit in range(level):
        partner = partner_2(gathered, "leaf", level_bit)
        upper_side = place >> level_bit & 1 == 1
        gathered = jnp.where(
            upper_side,
            jnp.concatenate([partner, gathered], axis=1),
            jnp.concatenate([gathered, partner], axis=1),
        )
    return gathered


def leaf_term(portion, matrix):
    return jnp.dot(portion, matrix, preferred_element_type=jnp.float32)


def per_device(
    right_side,
    send_order,
    owner_order,
    live_rows,
    lower_leaf,
    upper_leaf,
    lower_first,
    lower_second,
    lower_third,
    upper_first,
    upper_second,
    upper_third,
    downlink_first,
    downlink_second,
    downlink_third,
    uplink_first,
    uplink_second,
    uplink_third,
    pattern_first,
    pattern_second,
    pattern_third,
):
    fronts = lax.axis_size("front")
    leaves = lax.axis_size("leaf")
    place = lax.axis_index("leaf")
    column = lax.axis_index("front")
    columns = right_side.shape[0]
    leaf_rows = lower_leaf.shape[1]
    sep = lower_first.shape[0]
    lowers = [lower_first, lower_second, lower_third]
    uppers = [upper_first, upper_second, upper_third]
    downs = [downlink_first, downlink_second, downlink_third]
    backs = [uplink_first, uplink_second, uplink_third]
    patterns = [pattern_first, pattern_second, pattern_third]
    block = downlink_first.shape[0] // pattern_first.shape[0]
    pieces = [lower_first.shape[1], lower_second.shape[1], lower_third.shape[1]]
    starts = [0, leaves // 2, leaves // 2 + leaves // 4]
    outgoing = jnp.take(right_side, send_order, axis=1)
    arrived = lax.all_to_all(outgoing, ("leaf", "front"), split_axis=1, concat_axis=1, tiled=True)
    ordered = jnp.take(arrived, owner_order, axis=1)
    leaf_rhs = ordered[:, :leaf_rows]
    level_rhs = []
    offset = leaf_rows
    for level in range(1, 4):
        level_rhs.append(ordered[:, offset : offset + pieces[level - 1]])
        offset = offset + pieces[level - 1]
    piece_masks = []
    full_masks = []
    within = []
    for level in range(1, 4):
        group = 2**level
        member = place & group - 1
        node_live = lax.dynamic_index_in_dim(
            live_rows, starts[level - 1] + (place >> level), 0, keepdims=False
        )
        first_row = (member * fronts + column) * pieces[level - 1]
        piece_masks.append(
            (first_row + jnp.arange(pieces[level - 1], dtype=jnp.int32) < node_live).astype(
                jnp.float32
            )[None, :]
        )
        full_masks.append(
            (jnp.arange(sep, dtype=jnp.int32) < node_live).astype(jnp.float32)[None, :]
        )
        within.append(member)
    expanded = [spread(patterns[index], block) for index in range(3)]
    leaf_y = leaf_term(
        lax.all_gather(leaf_rhs, "front", axis=1, tiled=True), matrix=lower_leaf
    ).astype(jnp.bfloat16)
    children = leaf_y
    level_y = []
    for level in range(1, 4):
        group = 2**level
        piece = pieces[level - 1]
        member = within[level - 1]
        link = downs[level - 1] * expanded[level - 1]
        own_rhs = level_rhs[level - 1].astype(jnp.float32)
        shaped = link.reshape(group, fronts, piece, link.shape[1])
        term = jnp.einsum(
            "kc,jfpc->kfjp", children, shaped, preferred_element_type=jnp.float32
        ).reshape(columns, sep)
        first_row = (column * group + member) * piece
        current = lax.dynamic_slice_in_dim(term, first_row, piece, 1)
        term = lax.dynamic_update_slice_in_dim(term, current - own_rhs, first_row, 1)
        share = lax.psum_scatter(
            term.astype(jnp.bfloat16), "front", scatter_dimension=1, tiled=True
        ).astype(jnp.float32)
        for level_bit in reversed(range(level)):
            middle = share.shape[1] // 2
            lower_half = share[:, :middle]
            upper_half = share[:, middle:]
            high_side = place >> level_bit & 1 == 1
            keeping = jnp.where(high_side, upper_half, lower_half)
            sending = jnp.where(high_side, lower_half, upper_half)
            share = keeping + partner_2(sending.astype(jnp.bfloat16), "leaf", level_bit).astype(
                sending.dtype
            )
        reduced_piece = (-share * piece_masks[level - 1]).astype(jnp.bfloat16)
        reduced_full = collect_group(reduced_piece, level, place)
        solved = jnp.dot(reduced_full, lowers[level - 1], preferred_element_type=jnp.float32)
        found = (solved * piece_masks[level - 1]).astype(jnp.bfloat16)
        level_y.append(found)
        children = found
    level_x = [None, None, None]
    top_full = collect_group(level_y[2], 3, place)
    level_x[2] = (
        jnp.dot(top_full, upper_third, preferred_element_type=jnp.float32) * piece_masks[2]
    ).astype(jnp.bfloat16)
    for level in (2, 1):
        back = backs[level] * expanded[level]
        parent_full = collect_group(level_x[level], level + 1, place)
        update = level_y[level - 1].astype(jnp.float32) - jnp.dot(
            parent_full, back, preferred_element_type=jnp.float32
        )
        reduced = (update * piece_masks[level - 1]).astype(jnp.bfloat16)
        reduced_full = collect_group(reduced, level, place)
        solved = jnp.dot(reduced_full, uppers[level - 1], preferred_element_type=jnp.float32)
        level_x[level - 1] = (solved * piece_masks[level - 1]).astype(jnp.bfloat16)
    back = uplink_first * expanded[0]
    parent_full = collect_group(level_x[0], 1, place)
    update = (
        leaf_y.astype(jnp.float32) - jnp.dot(parent_full, back, preferred_element_type=jnp.float32)
    ).astype(jnp.bfloat16)
    leaf_x = leaf_term(
        lax.all_gather(update, "front", axis=1, tiled=True), matrix=upper_leaf
    ).astype(jnp.bfloat16)
    placed = jnp.concatenate([leaf_x, level_x[0], level_x[1], level_x[2]], axis=1)
    outbound = jnp.zeros_like(placed).at[:, owner_order].set(placed)
    returned = lax.all_to_all(outbound, ("leaf", "front"), split_axis=1, concat_axis=1, tiled=True)
    return jnp.zeros_like(returned).at[:, send_order].set(returned)


def solution(mesh):
    placed = (
        P(None, ("leaf", "front")),
        P(("leaf", "front")),
        P(("leaf", "front")),
        P(),
        P(None, ("leaf", "front")),
        P(None, ("leaf", "front")),
        P(None, ("leaf", "front")),
        P(None, ("leaf", "front")),
        P(None, ("leaf", "front")),
        P(None, ("leaf", "front")),
        P(None, ("leaf", "front")),
        P(None, ("leaf", "front")),
        P(None, ("leaf", "front")),
        P(None, ("leaf", "front")),
        P(None, ("leaf", "front")),
        P(None, ("leaf", "front")),
        P(None, ("leaf", "front")),
        P(None, ("leaf", "front")),
        P(None, ("leaf", "front")),
        P(None, ("leaf", "front")),
        P(None, ("leaf", "front")),
    )
    return jax.shard_map(
        per_device,
        mesh=mesh,
        in_specs=placed,
        out_specs=P(None, ("leaf", "front")),
        check_vma=False,
    )
```

profile of v0, /device:TPU:1, one launch (start us, length us, event | category | flops | bytes accessed | tf_op | source)
XLA Modules:
  0.0 459.3 jit_solution(6995919365814859507)
XLA Ops:
  9.0 2.0 gather_fusion
  12.0 11.5 %all-to-all-start = ((bf16[32,128,5]{0,2,1:T(8,128)(2,1)}), bf16[32,128,5]{0,2,1:T(8,128)(2,1)S(1)}, u32[]{:S(2)}, u32[]{:S(2)}) async-start(bf16[32,128,5]{0,2,1:T(8,128)(2,1)} %all_to_all.16), calls=%async_computation | async-start | bytes 524288 | tf_op jit(solution)/shard_map/all_to_all | solution.py:74
  25.8 3.3 bitcast_multiply_fusion.2
  30.7 3.8 all-to-all-done
  34.7 2.0 gather_fusion.1
  36.8 13.3 %all-gather = bf16[8,192,32]{1,2,0:T(8,128)(2,1)S(1)} all-gather(bf16[1,192,32]{1,2,0:T(8,128)(2,1)S(1)} %slice_bitcast_fusion), channel_id=1, replica_groups=mesh['leaf'=16,'front'=8] {'front'}, dimensions={0}, use_global_device_ids=true | all-gather | bytes 110592 | tf_op jit(solution)/shard_map/all_gather | solution.py:103
  50.6 2.0 fusion.2
  55.0 24.1 %reduce-scatter.4.cloned.1.call-done = bf16[32,512]{1,0:T(8,128)(2,1)} async-done(((bf16[32,4096]{1,0:T(8,128)(2,1)}), bf16[32,512]{1,0:T(8,128)(2,1)}) %reduce-scatter.4.cloned.1.call-update) | async-done | bytes 32784 | tf_op jit(solution)/shard_map/reduce_scatter | solution.py:120
  82.6 17.1 %all_gather.34 = bf16[32,2048]{1,0:T(8,128)(2,1)S(1)} all-gather(bf16[32,256]{1,0:T(8,128)(2,1)S(1)} %multiply_convert_fusion), channel_id=1, replica_groups=mesh['leaf'=16,'front'=8] {'front'}, dimensions={1}, use_global_device_ids=true | all-gather | bytes 147456 | tf_op jit(solution)/shard_map/all_gather | solution.py:19
  100.9 4.1 copy.74
  105.0 4.2 copy.84
  109.4 4.5 bitcast_multiply_fusion
  113.9 4.1 copy.91
  121.8 27.1 %reduce-scatter.6.cloned.1.call-done = bf16[32,512]{1,0:T(8,128)(2,1)} async-done(((bf16[32,4096]{1,0:T(8,128)(2,1)}), bf16[32,512]{1,0:T(8,128)(2,1)}) %reduce-scatter.6.cloned.1.call-update) | async-done | bytes 32784 | tf_op jit(solution)/shard_map/reduce_scatter | solution.py:120
  149.6 3.0 collective-permute-start.2
  156.4 16.6 %all_gather.35 = bf16[32,1024]{1,0:T(8,128)(2,1)S(1)} all-gather(bf16[32,128]{1,0:T(8,128)(2,1)S(1)} %multiply_convert_fusion.2), channel_id=1, replica_groups=mesh['leaf'=16,'front'=8] {'front'}, dimensions={1}, use_global_device_ids=true | all-gather | bytes 73728 | tf_op jit(solution)/shard_map/all_gather | solution.py:19
  174.3 2.2 collective-permute-done.4
  176.5 3.1 collective-permute-start.5
  181.1 2.3 copy.83
  183.6 2.7 bitcast_multiply_fusion.4
  196.3 27.5 %reduce-scatter.8.cloned.1.call-done = bf16[32,512]{1,0:T(8,128)(2,1)} async-done(((bf16[32,4096]{1,0:T(8,128)(2,1)}), bf16[32,512]{1,0:T(8,128)(2,1)}) %reduce-scatter.8.cloned.1.call-update) | async-done | bytes 32784 | tf_op jit(solution)/shard_map/reduce_scatter | solution.py:120
  227.3 2.9 collective-permute-start.7
  234.0 19.3 %all-gather.1 = bf16[8,64,32]{1,2,0:T(8,128)(2,1)S(1)} all-gather(bf16[1,64,32]{1,2,0:T(8,128)(2,1)S(1)} %fusion.79), channel_id=1, replica_groups=mesh['leaf'=16,'front'=8] {'front'}, dimensions={0}, use_global_device_ids=true | all-gather | bytes 36864 | tf_op jit(solution)/shard_map/all_gather | solution.py:19
  256.4 2.8 collective-permute-start.10
  259.2 1.9 collective-permute-done.10
  262.5 2.5 collective-permute-done.11
  266.3 16.2 %all-gather.2 = bf16[8,64,32]{1,2,0:T(8,128)(2,1)S(1)} all-gather(bf16[1,64,32]{1,2,0:T(8,128)(2,1)S(1)} %fusion.17), channel_id=1, replica_groups=mesh['leaf'=16,'front'=8] {'front'}, dimensions={0}, use_global_device_ids=true | all-gather | bytes 36864 | tf_op jit(solution)/shard_map/all_gather | solution.py:19
  285.5 2.8 collective-permute-start.13
  291.6 2.5 collective-permute-done.14
  295.5 16.2 %all-gather.3 = bf16[8,64,32]{1,2,0:T(8,128)(2,1)S(1)} all-gather(bf16[1,64,32]{1,2,0:T(8,128)(2,1)S(1)} %bitcast.122), channel_id=1, replica_groups=mesh['leaf'=16,'front'=8] {'front'}, dimensions={0}, use_global_device_ids=true | all-gather | bytes 36864 | tf_op jit(solution)/shard_map/all_gather | solution.py:19
  314.7 2.8 collective-permute-start.16
  320.8 2.5 collective-permute-done.17
  323.8 14.7 %all_gather.39 = bf16[32,1024]{1,0:T(8,128)(2,1)S(1)} all-gather(bf16[32,128]{1,0:T(8,128)(2,1)S(1)} %fusion.12), channel_id=1, replica_groups=mesh['leaf'=16,'front'=8] {'front'}, dimensions={1}, use_global_device_ids=true | all-gather | bytes 73728 | tf_op jit(solution)/shard_map/all_gather | solution.py:19
  339.6 2.4 collective-permute-done.18
  342.0 2.8 collective-permute-start.19
  344.8 2.6 collective-permute-done.19
  347.8 13.1 %all_gather.40 = bf16[32,1024]{1,0:T(8,128)(2,1)S(1)} all-gather(bf16[32,128]{1,0:T(8,128)(2,1)S(1)} %fusion.16), channel_id=1, replica_groups=mesh['leaf'=16,'front'=8] {'front'}, dimensions={1}, use_global_device_ids=true | all-gather | bytes 73728 | tf_op jit(solution)/shard_map/all_gather | solution.py:19
  362.1 2.4 collective-permute-done.20
  364.5 2.8 collective-permute-start.21
  367.2 2.6 collective-permute-done.21
  370.6 14.9 %all_gather.41 = bf16[32,2048]{1,0:T(8,128)(2,1)S(1)} all-gather(bf16[32,256]{1,0:T(8,128)(2,1)S(1)} %fusion.8), channel_id=1, replica_groups=mesh['leaf'=16,'front'=8] {'front'}, dimensions={1}, use_global_device_ids=true | all-gather | bytes 147456 | tf_op jit(solution)/shard_map/all_gather | solution.py:19
  386.7 3.8 collective-permute-done.22
  390.9 13.6 %all_gather.42 = bf16[32,2048]{1,0:T(8,128)(2,1)S(1)} all-gather(bf16[32,256]{1,0:T(8,128)(2,1)S(1)} %fusion.9), channel_id=1, replica_groups=mesh['leaf'=16,'front'=8] {'front'}, dimensions={1}, use_global_device_ids=true | all-gather | bytes 147456 | tf_op jit(solution)/shard_map/all_gather | solution.py:19
  405.7 3.8 collective-permute-done.23
  410.1 13.6 %all-gather.4 = bf16[8,192,32]{1,2,0:T(8,128)(2,1)S(1)} all-gather(bf16[1,192,32]{1,2,0:T(8,128)(2,1)S(1)} %fusion.10), channel_id=1, replica_groups=mesh['leaf'=16,'front'=8] {'front'}, dimensions={0}, use_global_device_ids=true | all-gather | bytes 110592 | tf_op jit(solution)/shard_map/all_gather | solution.py:160
  424.4 4.3 scatter_custom_fusion
  428.8 18.5 %all_to_all.24 = bf16[32,128,5]{0,2,1:T(8,128)(2,1)S(1)} all-to-all(bf16[32,128,5]{0,2,1:T(8,128)(2,1)S(1)} %all_to_all.19), channel_id=1, replica_groups=mesh['leaf'=16,'front'=8] {'leaf','front'}, dimensions={1} | all-to-all | bytes 81920 | tf_op jit(solution)/shard_map/all_to_all | solution.py:164
  447.4 4.6 %scatter_custom_fusion.1 = bf16[32,640]{0,1:T(8,128)(2,1)S(1)} fusion(s32[640]{0:T(1024)S(1)} %compare_select_fusion.1, bf16[32,640]{0,1:T(8,128)(2,1)S(1)} %reshape.88, bf16[]{:T(256)} %constant.15.clone.1), kind=kCustom, calls=%fused_computation.102 | custom fusion | bytes 204802 | tf_op jit(solution)/shard_map/scatter | solution.py:165
  (153 shorter events, 72.4 us)
Async XLA Ops:
  6.5 111.5 %copy-start = (bf16[4096,256]{1,0:T(8,128)(2,1)S(1)}, bf16[4096,256]{1,0:T(8,128)(2,1)}, u32[]{:S(2)}) copy-start(bf16[4096,256]{1,0:T(8,128)(2,1)} %param.29) | copy-start | bytes 6291460
  12.0 22.6 %all-to-all-start = ((bf16[32,128,5]{0,2,1:T(8,128)(2,1)}), bf16[32,128,5]{0,2,1:T(8,128)(2,1)S(1)}, u32[]{:S(2)}, u32[]{:S(2)}) async-start(bf16[32,128,5]{0,2,1:T(8,128)(2,1)} %all_to_all.16), calls=%async_computation | async-start | bytes 524288 | tf_op jit(solution)/shard_map/all_to_all | solution.py:74
  23.5 55.7 %reduce-scatter.4.cloned.1.call-start = ((), (), s32[]{:S(2)}) async-start(), calls=%async_computation.5 | async-start | bytes 294912 | tf_op jit(solution)/shard_map/reduce_scatter | solution.py:120
  29.1 21.2 %copy-start.6 = (bf16[1536,192]{0,1:T(8,128)(2,1)S(1)}, bf16[1536,192]{0,1:T(8,128)(2,1)}, u32[]{:S(2)}) copy-start(bf16[1536,192]{0,1:T(8,128)(2,1)} %param.27) | copy-start | bytes 1769476
  52.6 1.7 copy-start.8
  54.3 94.5 %reduce-scatter.6.cloned.1.call-start = ((), (), s32[]{:S(2)}) async-start(), calls=%async_computation.6 | async-start | bytes 294912 | tf_op jit(solution)/shard_map/reduce_scatter | solution.py:120
  79.9 2.7 collective-permute-start
  99.7 18.3 %collective-permute-start.1 = (bf16[32,2048]{1,0:T(8,128)(2,1)S(1)}, bf16[32,2048]{1,0:T(8,128)(2,1)S(1)}, u32[]{:S(2)}, u32[]{:S(2)}) collective-permute-start(bf16[32,2048]{1,0:T(8,128)(2,1)S(1)} %all_gather.34), channel_id=1, source_target_pairs={{0,8},{8,0},{16,24},{24,16},{32,40},{40,32},{48,56},{56,48},{64,72... | collective-permute-start | bytes 393224 | tf_op jit(solution)/shard_map/ppermute | solution.py:10
  105.0 4.2 copy-start.9
  118.0 1.6 copy-start.1
  121.7 102.1 %reduce-scatter.8.cloned.1.call-start = ((), (), s32[]{:S(2)}) async-start(), calls=%async_computation.7 | async-start | bytes 294912 | tf_op jit(solution)/shard_map/reduce_scatter | solution.py:120
  149.6 4.2 collective-permute-start.2
  153.8 2.6 collective-permute-start.3
  173.0 3.5 collective-permute-start.4
  176.5 11.4 %collective-permute-start.5 = (bf16[32,2048]{1,0:T(8,128)(2,1)S(1)}, bf16[32,2048]{1,0:T(8,128)(2,1)S(1)}, u32[]{:S(2)}, u32[]{:S(2)}) collective-permute-start(bf16[32,2048]{1,0:T(8,128)(2,1)S(1)} %maximum_select_fusion.18), channel_id=1, source_target_pairs={{0,16},{8,24},{16,0},{24,8},{32,48},{40,56},{48,32},{56,40},{64,80... | collective-permute-start | bytes 393224 | tf_op jit(solution)/shard_map/ppermute | solution.py:10
  179.6 3.8 copy-start.11
  224.6 2.7 collective-permute-start.6
  227.3 4.1 collective-permute-start.7
  231.4 2.5 collective-permute-start.8
  253.5 2.8 collective-permute-start.9
  256.4 4.7 %collective-permute-start.10 = (bf16[32,1024]{1,0:T(8,128)(2,1)S(1)}, bf16[32,1024]{1,0:T(8,128)(2,1)S(1)}, u32[]{:S(2)}, u32[]{:S(2)}) collective-permute-start(bf16[32,1024]{1,0:T(8,128)(2,1)S(1)} %maximum_select_fusion.24), channel_id=1, source_target_pairs={{0,16},{8,24},{16,0},{24,8},{32,48},{40,56},{48,32},{56,40},{64,80... | collective-permute-start | bytes 196616 | tf_op jit(solution)/shard_map/ppermute | solution.py:10
  261.1 62.2 %copy-start.5 = (bf16[4096,128]{0,1:T(8,128)(2,1)S(1)}, bf16[4096,128]{0,1:T(8,128)(2,1)}, u32[]{:S(2)}) copy-start(bf16[4096,128]{0,1:T(8,128)(2,1)} %get-tuple-element.10) | copy-start | bytes 3145732
  261.1 3.9 collective-permute-start.11
  282.7 2.8 collective-permute-start.12
  285.5 4.7 %collective-permute-start.13 = (bf16[32,1024]{1,0:T(8,128)(2,1)S(1)}, bf16[32,1024]{1,0:T(8,128)(2,1)S(1)}, u32[]{:S(2)}, u32[]{:S(2)}) collective-permute-start(bf16[32,1024]{1,0:T(8,128)(2,1)S(1)} %maximum_select_fusion.25), channel_id=1, source_target_pairs={{0,16},{8,24},{16,0},{24,8},{32,48},{40,56},{48,32},{56,40},{64,80... | collective-permute-start | bytes 196616 | tf_op jit(solution)/shard_map/ppermute | solution.py:10
  290.3 3.9 collective-permute-start.14
  311.8 35.6 %copy-start.10 = (bf16[4096,128]{1,0:T(8,128)(2,1)S(1)}, bf16[4096,128]{1,0:T(8,128)(2,1)}, u32[]{:S(2)}) copy-start(bf16[4096,128]{1,0:T(8,128)(2,1)} %param.33) | copy-start | bytes 3145732
  311.8 2.8 collective-permute-start.15
  314.7 55.2 %copy-start.2 = (bf16[4096,256]{0,1:T(8,128)(2,1)S(1)}, bf16[4096,256]{0,1:T(8,128)(2,1)}, u32[]{:S(2)}) copy-start(bf16[4096,256]{0,1:T(8,128)(2,1)} %get-tuple-element.8) | copy-start | bytes 6291460
  314.7 4.7 %collective-permute-start.16 = (bf16[32,1024]{1,0:T(8,128)(2,1)S(1)}, bf16[32,1024]{1,0:T(8,128)(2,1)S(1)}, u32[]{:S(2)}, u32[]{:S(2)}) collective-permute-start(bf16[32,1024]{1,0:T(8,128)(2,1)S(1)} %maximum_select_fusion.26), channel_id=1, source_target_pairs={{0,16},{8,24},{16,0},{24,8},{32,48},{40,56},{48,32},{56,40},{64,80... | collective-permute-start | bytes 196616 | tf_op jit(solution)/shard_map/ppermute | solution.py:10
  319.5 3.9 collective-permute-start.17
  338.5 3.5 collective-permute-start.18
  342.0 48.5 %copy-start.3 = (bf16[4096,256]{1,0:T(8,128)(2,1)S(1)}, bf16[4096,256]{1,0:T(8,128)(2,1)}, u32[]{:S(2)}) copy-start(bf16[4096,256]{1,0:T(8,128)(2,1)} %param.32) | copy-start | bytes 6291460
  342.0 5.4 %collective-permute-start.19 = (bf16[32,2048]{1,0:T(8,128)(2,1)S(1)}, bf16[32,2048]{1,0:T(8,128)(2,1)S(1)}, u32[]{:S(2)}, u32[]{:S(2)}) collective-permute-start(bf16[32,2048]{1,0:T(8,128)(2,1)S(1)} %maximum_select_fusion.22), channel_id=1, source_target_pairs={{0,16},{8,24},{16,0},{24,8},{32,48},{40,56},{48,32},{56,40},{64,80... | collective-permute-start | bytes 393224 | tf_op jit(solution)/shard_map/ppermute | solution.py:10
  360.9 3.5 collective-permute-start.20
  364.5 5.4 %collective-permute-start.21 = (bf16[32,2048]{1,0:T(8,128)(2,1)S(1)}, bf16[32,2048]{1,0:T(8,128)(2,1)S(1)}, u32[]{:S(2)}, u32[]{:S(2)}) collective-permute-start(bf16[32,2048]{1,0:T(8,128)(2,1)S(1)} %maximum_select_fusion.23), channel_id=1, source_target_pairs={{0,16},{8,24},{16,0},{24,8},{32,48},{40,56},{48,32},{56,40},{64,80... | collective-permute-start | bytes 393224 | tf_op jit(solution)/shard_map/ppermute | solution.py:10
  369.9 39.6 %copy-start.4 = (bf16[4096,192]{0,1:T(8,128)(2,1)S(1)}, bf16[4096,192]{0,1:T(8,128)(2,1)}, u32[]{:S(2)}) copy-start(bf16[4096,192]{0,1:T(8,128)(2,1)} %get-tuple-element.6) | copy-start | bytes 4718596
  385.6 38.3 %copy-start.7 = (bf16[1536,192]{0,1:T(8,128)(2,1)S(1)}, bf16[1536,192]{0,1:T(8,128)(2,1)}, u32[]{:S(2)}) copy-start(bf16[1536,192]{0,1:T(8,128)(2,1)} %param.28) | copy-start | bytes 1769476
  385.6 4.9 %collective-permute-start.22 = (bf16[32,2048]{1,0:T(8,128)(2,1)S(1)}, bf16[32,2048]{1,0:T(8,128)(2,1)S(1)}, u32[]{:S(2)}, u32[]{:S(2)}) collective-permute-start(bf16[32,2048]{1,0:T(8,128)(2,1)S(1)} %all_gather.41), channel_id=1, source_target_pairs={{0,8},{8,0},{16,24},{24,16},{32,40},{40,32},{48,56},{56,48},{64,72... | collective-permute-start | bytes 393224 | tf_op jit(solution)/shard_map/ppermute | solution.py:10
  404.5 4.9 %collective-permute-start.23 = (bf16[32,2048]{1,0:T(8,128)(2,1)S(1)}, bf16[32,2048]{1,0:T(8,128)(2,1)S(1)}, u32[]{:S(2)}, u32[]{:S(2)}) collective-permute-start(bf16[32,2048]{1,0:T(8,128)(2,1)S(1)} %all_gather.42), channel_id=1, source_target_pairs={{0,8},{8,0},{16,24},{24,16},{32,40},{40,32},{48,56},{56,48},{64,72... | collective-permute-start | bytes 393224 | tf_op jit(solution)/shard_map/ppermute | solution.py:10
Sparse Core Ops, SparseCore 0:
  54.4 24.6 reduce-scatter.3
  121.8 26.9 reduce-scatter.5
  196.4 27.3 reduce-scatter.7
where the time goes:
time: 461 us; the launch traced here: 459 us
  blocking collectives  187 us (41%)
  waiting for transfers between devices  126 us (27%)
  starting transfers between devices  55 us (12%)
  local copies, waits for them, and re-layouts  43.1 us (9%)
  other arithmetic  23.3 us (5%)
  between operations  13.6 us (3%)
  matrix products  11.4 us (2%)
    all_gather x9, blocking collectives, collect_group(): gathered = lax.all_gather(portion, 'front', axis=1, tiled=True)  142 us
    reduce_scatter x3, waiting for transfers between devices, per_device(): lax.psum_scatter(term.astype(jnp.bfloat16), 'front', scatter_dimension=1,...  78.7 us
    ppermute x24, starting transfers between devices, partner_2(): return lax.ppermute(value, axis, pairs)  43.4 us
    ppermute x24, waiting for transfers between devices, partner_2(): return lax.ppermute(value, axis, pairs)  43.3 us
    all_to_all x1, blocking collectives, per_device(): lax.all_to_all(outbound, ('leaf', 'front'), split_axis=1, concat_axis=1,...  18.5 us
    unnamed x36, local copies, waits for them, and re-layouts  16.5 us
    all_gather x1, blocking collectives, per_device(): lax.all_gather(update, 'front', axis=1, tiled=True)  13.6 us
    all_gather x1, blocking collectives, per_device(): lax.all_gather(leaf_rhs, 'front', axis=1, tiled=True)  13.3 us
  transfers between devices with their start and end apart: 28, of which 26 were waited for; matrix products, arithmetic and copies ran while one was open for 8% of the time, Pallas kernels for 0%

commit v1 on v0

--- a/solution.py
+++ b/solution.py
@@ -16,7 +16,8 @@
 
 
 def collect_group(portion, level, place):
-    gathered = lax.all_gather(portion, "front", axis=1, tiled=True)
+    outgoing_2 = jnp.stack([portion] * lax.axis_size("front"))
+    gathered = jnp.concatenate(lax.all_to_all(outgoing_2, "front", 0, 0), axis=1)
     for level_bit in range(level):
         partner = partner_2(gathered, "leaf", level_bit)
         upper_side = place >> level_bit & 1 == 1

time: 461 us -> 422 us (0.915)
  blocking collectives: 187 us -> 150 us
    all_gather x9 -> x0, blocking collectives: 142 us -> none  [collect_group(): gathered = lax.all_gather(portion, 'front', axis=1, tiled=True)]
    all_to_all x0 -> x9, blocking collectives: none -> 104 us  [collect_group(): lax.all_to_all(outgoing_2, 'front', 0, 0)]
    unnamed x36 -> x39, local copies, waits for them, and re-layouts: 16.5 us -> 16.8 us
where the time goes in v1:
time: 422 us; the launch traced here: 421 us
  blocking collectives  150 us (36%)
  waiting for transfers between devices  124 us (29%)
  starting transfers between devices  54.4 us (13%)
  local copies, waits for them, and re-layouts  44 us (10%)
  other arithmetic  23.3 us (6%)
  between operations  13.7 us (3%)
  matrix products  11.5 us (3%)
    all_to_all x9, blocking collectives, collect_group(): lax.all_to_all(outgoing_2, 'front', 0, 0)  104 us
    reduce_scatter x3, waiting for transfers between devices, per_device(): lax.psum_scatter(term.astype(jnp.bfloat16), 'front', scatter_dimension=1,...  78.9 us
    ppermute x24, starting transfers between devices, partner_2(): return lax.ppermute(value, axis, pairs)  42.7 us
    ppermute x24, waiting for transfers between devices, partner_2(): return lax.ppermute(value, axis, pairs)  41.2 us
    all_to_all x1, blocking collectives, per_device(): lax.all_to_all(outbound, ('leaf', 'front'), split_axis=1, concat_axis=1,...  18.5 us
    unnamed x39, local copies, waits for them, and re-layouts  16.8 us
    all_gather x1, blocking collectives, per_device(): lax.all_gather(update, 'front', axis=1, tiled=True)  14.6 us
    all_gather x1, blocking collectives, per_device(): lax.all_gather(leaf_rhs, 'front', axis=1, tiled=True)  13.3 us
  transfers between devices with their start and end apart: 28, of which 26 were waited for; matrix products, arithmetic and copies ran while one was open for 8% of the time, Pallas kernels for 0%

profile of v1, /device:TPU:1, one launch (start us, length us, event | category | flops | bytes accessed | tf_op | source)
XLA Modules:
  0.0 420.9 jit_solution(3300213880173162304)
XLA Ops:
  9.0 2.0 gather_fusion
  12.0 11.5 %all-to-all-start = ((bf16[32,128,5]{0,2,1:T(8,128)(2,1)}), bf16[32,128,5]{0,2,1:T(8,128)(2,1)S(1)}, u32[]{:S(2)}, u32[]{:S(2)}) async-start(bf16[32,128,5]{0,2,1:T(8,128)(2,1)} %all_to_all.43), calls=%async_computation | async-start | bytes 524288 | tf_op jit(solution)/shard_map/all_to_all | solution.py:75
  25.8 3.3 bitcast_multiply_fusion.2
  30.7 3.8 all-to-all-done
  36.8 13.3 %all-gather = bf16[8,192,32]{1,2,0:T(8,128)(2,1)S(1)} all-gather(bf16[1,192,32]{1,2,0:T(8,128)(2,1)S(1)} %slice_bitcast_fusion), channel_id=1, replica_groups=mesh['leaf'=16,'front'=8] {'front'}, dimensions={0}, use_global_device_ids=true | all-gather | bytes 110592 | tf_op jit(solution)/shard_map/all_gather | solution.py:104
  50.6 2.0 fusion.2
  55.0 24.1 %reduce-scatter.4.cloned.1.call-done = bf16[32,512]{1,0:T(8,128)(2,1)} async-done(((bf16[32,4096]{1,0:T(8,128)(2,1)}), bf16[32,512]{1,0:T(8,128)(2,1)}) %reduce-scatter.4.cloned.1.call-update) | async-done | bytes 32784 | tf_op jit(solution)/shard_map/reduce_scatter | solution.py:121
  82.6 12.1 %all_to_all.69 = bf16[8,32,256]{2,1,0:T(8,128)(2,1)S(1)} all-to-all(bf16[8,32,256]{2,1,0:T(8,128)(2,1)S(1)} %stack.18), channel_id=1, replica_groups=mesh['leaf'=16,'front'=8] {'front'}, dimensions={0} | all-to-all | bytes 262144 | tf_op jit(solution)/shard_map/all_to_all | solution.py:20
  96.0 4.1 copy.85
  100.2 4.2 copy.98
  104.6 4.5 %bitcast_multiply_fusion = (bf16[4096,256]{0,1:T(8,128)(2,1)}, bf16[4096,256]{0,1:T(8,128)(2,1)}) fusion(bf16[4096,256]{0,1:T(8,128)(2,1)} %copy.98, bf16[4096,4]{0,1:T(4,128)(2,1)S(1)} %convert_element_type.183, bf16[4096,256]{0,1:T(8,128)(2,1)} %copy.85), kind=kLoop, calls=%fused_computation.4 | loop fusion | flops 2097152 | bytes 8421376 | tf_op jit(solution)/shard_map/mul | solution.py:146
  109.1 4.1 copy.107
  116.9 27.5 %reduce-scatter.6.cloned.1.call-done = bf16[32,512]{1,0:T(8,128)(2,1)} async-done(((bf16[32,4096]{1,0:T(8,128)(2,1)}), bf16[32,512]{1,0:T(8,128)(2,1)}) %reduce-scatter.6.cloned.1.call-update) | async-done | bytes 32784 | tf_op jit(solution)/shard_map/reduce_scatter | solution.py:121
  145.2 2.9 collective-permute-start.2
  152.0 12.8 %all_to_all.70 = bf16[8,32,128]{2,1,0:T(8,128)(2,1)S(1)} all-to-all(bf16[8,32,128]{2,1,0:T(8,128)(2,1)S(1)} %stack.19), channel_id=1, replica_groups=mesh['leaf'=16,'front'=8] {'front'}, dimensions={0} | all-to-all | bytes 131072 | tf_op jit(solution)/shard_map/all_to_all | solution.py:20
  168.0 3.0 collective-permute-start.5
  172.5 2.3 copy.95
  175.0 2.7 bitcast_multiply_fusion.4
  187.8 27.3 %reduce-scatter.8.cloned.1.call-done = bf16[32,512]{1,0:T(8,128)(2,1)} async-done(((bf16[32,4096]{1,0:T(8,128)(2,1)}), bf16[32,512]{1,0:T(8,128)(2,1)}) %reduce-scatter.8.cloned.1.call-update) | async-done | bytes 32784 | tf_op jit(solution)/shard_map/reduce_scatter | solution.py:121
  218.5 2.9 collective-permute-start.7
  225.4 13.9 %all_to_all.71 = bf16[8,2,1024]{2,1,0:T(2,128)(2,1)S(1)} all-to-all(bf16[8,2,1024]{2,1,0:T(2,128)(2,1)S(1)} %reshape.204), channel_id=1, replica_groups=mesh['leaf'=16,'front'=8] {'front'}, dimensions={0} | all-to-all | bytes 65536 | tf_op jit(solution)/shard_map/all_to_all | solution.py:20
  242.5 2.7 collective-permute-start.10
  245.2 2.0 collective-permute-done.10
  248.6 2.6 collective-permute-done.11
  252.6 11.3 %all_to_all.72 = bf16[8,2,1024]{2,1,0:T(2,128)(2,1)S(1)} all-to-all(bf16[8,2,1024]{2,1,0:T(2,128)(2,1)S(1)} %reshape.206), channel_id=1, replica_groups=mesh['leaf'=16,'front'=8] {'front'}, dimensions={0} | all-to-all | bytes 65536 | tf_op jit(solution)/shard_map/all_to_all | solution.py:20
  267.0 2.7 collective-permute-start.13
  269.7 2.0 collective-permute-done.13
  273.0 2.6 collective-permute-done.14
  277.0 11.3 %all_to_all.73 = bf16[8,2,1024]{2,1,0:T(2,128)(2,1)S(1)} all-to-all(bf16[8,2,1024]{2,1,0:T(2,128)(2,1)S(1)} %reshape.208), channel_id=1, replica_groups=mesh['leaf'=16,'front'=8] {'front'}, dimensions={0} | all-to-all | bytes 65536 | tf_op jit(solution)/shard_map/all_to_all | solution.py:20
  291.4 2.7 collective-permute-start.16
  294.2 2.0 collective-permute-done.16
  297.5 2.6 collective-permute-done.17
  300.6 11.5 %all_to_all.74 = bf16[8,32,128]{2,1,0:T(8,128)(2,1)S(1)} all-to-all(bf16[8,32,128]{2,1,0:T(8,128)(2,1)S(1)} %stack.23), channel_id=1, replica_groups=mesh['leaf'=16,'front'=8] {'front'}, dimensions={0} | all-to-all | bytes 131072 | tf_op jit(solution)/shard_map/all_to_all | solution.py:20
  313.2 2.0 collective-permute-done.18
  315.3 2.7 collective-permute-start.19
  318.0 2.7 collective-permute-done.19
  321.0 10.4 %all_to_all.75 = bf16[8,32,128]{2,1,0:T(8,128)(2,1)S(1)} all-to-all(bf16[8,32,128]{2,1,0:T(8,128)(2,1)S(1)} %stack.24), channel_id=1, replica_groups=mesh['leaf'=16,'front'=8] {'front'}, dimensions={0} | all-to-all | bytes 131072 | tf_op jit(solution)/shard_map/all_to_all | solution.py:20
  332.6 2.0 collective-permute-done.20
  334.6 2.7 collective-permute-start.21
  337.3 2.7 collective-permute-done.21
  340.8 10.9 %all_to_all.76 = bf16[8,32,256]{2,1,0:T(8,128)(2,1)S(1)} all-to-all(bf16[8,32,256]{2,1,0:T(8,128)(2,1)S(1)} %stack.25), channel_id=1, replica_groups=mesh['leaf'=16,'front'=8] {'front'}, dimensions={0} | all-to-all | bytes 262144 | tf_op jit(solution)/shard_map/all_to_all | solution.py:20
  352.8 3.0 collective-permute-done.22
  356.3 9.6 %all_to_all.77 = bf16[8,32,256]{2,1,0:T(8,128)(2,1)S(1)} all-to-all(bf16[8,32,256]{2,1,0:T(8,128)(2,1)S(1)} %stack.26), channel_id=1, replica_groups=mesh['leaf'=16,'front'=8] {'front'}, dimensions={0} | all-to-all | bytes 262144 | tf_op jit(solution)/shard_map/all_to_all | solution.py:20
  367.1 3.0 collective-permute-done.23
  370.7 14.6 %all-gather.1 = bf16[8,192,32]{1,2,0:T(8,128)(2,1)S(1)} all-gather(bf16[1,192,32]{1,2,0:T(8,128)(2,1)S(1)} %fusion.10), channel_id=1, replica_groups=mesh['leaf'=16,'front'=8] {'front'}, dimensions={0}, use_global_device_ids=true | all-gather | bytes 110592 | tf_op jit(solution)/shard_map/all_gather | solution.py:161
  386.1 4.3 %scatter_custom_fusion = bf16[32,640]{0,1:T(8,128)(2,1)S(1)} fusion(s32[640]{0:T(1024)S(1)} %compare_select_fusion, bf16[640,32]{1,0:T(8,128)(2,1)S(1)} %copy.102, bf16[]{:T(256)} %constant.15.clone.1), kind=kCustom, calls=%fused_computation.111 | custom fusion | bytes 40962 | tf_op jit(solution)/shard_map/scatter | solution.py:164
  390.4 18.5 %all_to_all.78 = bf16[32,128,5]{0,2,1:T(8,128)(2,1)S(1)} all-to-all(bf16[32,128,5]{0,2,1:T(8,128)(2,1)S(1)} %all_to_all.55), channel_id=1, replica_groups=mesh['leaf'=16,'front'=8] {'leaf','front'}, dimensions={1} | all-to-all | bytes 81920 | tf_op jit(solution)/shard_map/all_to_all | solution.py:165
  409.0 4.6 %scatter_custom_fusion.1 = bf16[32,640]{0,1:T(8,128)(2,1)S(1)} fusion(s32[640]{0:T(1024)S(1)} %compare_select_fusion.1, bf16[32,640]{0,1:T(8,128)(2,1)S(1)} %reshape.178, bf16[]{:T(256)} %constant.15.clone.1), kind=kCustom, calls=%fused_computation.101 | custom fusion | bytes 204802 | tf_op jit(solution)/shard_map/scatter | solution.py:166
  (174 shorter events, 73.3 us)
Async XLA Ops:
  6.5 106.6 %copy-start = (bf16[4096,256]{1,0:T(8,128)(2,1)S(1)}, bf16[4096,256]{1,0:T(8,128)(2,1)}, u32[]{:S(2)}) copy-start(bf16[4096,256]{1,0:T(8,128)(2,1)} %param.29) | copy-start | bytes 6291460
  12.0 22.6 %all-to-all-start = ((bf16[32,128,5]{0,2,1:T(8,128)(2,1)}), bf16[32,128,5]{0,2,1:T(8,128)(2,1)S(1)}, u32[]{:S(2)}, u32[]{:S(2)}) async-start(bf16[32,128,5]{0,2,1:T(8,128)(2,1)} %all_to_all.43), calls=%async_computation | async-start | bytes 524288 | tf_op jit(solution)/shard_map/all_to_all | solution.py:75
  23.5 55.7 %reduce-scatter.4.cloned.1.call-start = ((), (), s32[]{:S(2)}) async-start(), calls=%async_computation.14 | async-start | bytes 294912 | tf_op jit(solution)/shard_map/reduce_scatter | solution.py:121
  29.1 21.2 %copy-start.6 = (bf16[1536,192]{0,1:T(8,128)(2,1)S(1)}, bf16[1536,192]{0,1:T(8,128)(2,1)}, u32[]{:S(2)}) copy-start(bf16[1536,192]{0,1:T(8,128)(2,1)} %param.27) | copy-start | bytes 1769476
  52.6 1.7 copy-start.8
  54.3 90.1 %reduce-scatter.6.cloned.1.call-start = ((), (), s32[]{:S(2)}) async-start(), calls=%async_computation.15 | async-start | bytes 294912 | tf_op jit(solution)/shard_map/reduce_scatter | solution.py:121
  79.9 2.7 collective-permute-start
  94.8 18.4 %collective-permute-start.1 = (bf16[32,2048]{1,0:T(8,128)(2,1)S(1)}, bf16[32,2048]{1,0:T(8,128)(2,1)S(1)}, u32[]{:S(2)}, u32[]{:S(2)}) collective-permute-start(bf16[32,2048]{1,0:T(8,128)(2,1)S(1)} %bitcast.126), channel_id=1, source_target_pairs={{0,8},{8,0},{16,24},{24,16},{32,40},{40,32},{48,56},{56,48},{64,72... | collective-permute-start | bytes 393224 | tf_op jit(solution)/shard_map/ppermute | solution.py:10
  100.2 4.2 copy-start.9
  113.1 1.6 copy-start.1
  116.9 98.2 %reduce-scatter.8.cloned.1.call-start = ((), (), s32[]{:S(2)}) async-start(), calls=%async_computation.16 | async-start | bytes 294912 | tf_op jit(solution)/shard_map/reduce_scatter | solution.py:121
  145.2 4.2 collective-permute-start.2
  149.4 2.6 collective-permute-start.3
  164.8 3.1 collective-permute-start.4
  168.0 11.3 %collective-permute-start.5 = (bf16[32,2048]{1,0:T(8,128)(2,1)S(1)}, bf16[32,2048]{1,0:T(8,128)(2,1)}, u32[]{:S(2)}, u32[]{:S(2)}) collective-permute-start(bf16[32,2048]{1,0:T(8,128)(2,1)S(1)} %maximum_select_fusion.18), channel_id=1, source_target_pairs={{0,16},{8,24},{16,0},{24,8},{32,48},{40,56},{48,32},{56,40},{64,80... | collective-permute-start | bytes 393224 | tf_op jit(solution)/shard_map/ppermute | solution.py:10
  171.0 3.8 copy-start.11
  215.8 2.7 collective-permute-start.6
  218.5 4.1 collective-permute-start.7
  222.7 2.5 collective-permute-start.8
  239.6 2.8 collective-permute-start.9
  242.5 4.7 %collective-permute-start.10 = (bf16[32,1024]{1,0:T(8,128)(2,1)S(1)}, bf16[32,1024]{1,0:T(8,128)(2,1)S(1)}, u32[]{:S(2)}, u32[]{:S(2)}) collective-permute-start(bf16[32,1024]{1,0:T(8,128)(2,1)S(1)} %maximum_select_fusion.24), channel_id=1, source_target_pairs={{0,16},{8,24},{16,0},{24,8},{32,48},{40,56},{48,32},{56,40},{64,80... | collective-permute-start | bytes 196616 | tf_op jit(solution)/shard_map/ppermute | solution.py:10
  247.2 52.9 %copy-start.5 = (bf16[4096,128]{0,1:T(8,128)(2,1)S(1)}, bf16[4096,128]{0,1:T(8,128)(2,1)}, u32[]{:S(2)}) copy-start(bf16[4096,128]{0,1:T(8,128)(2,1)} %get-tuple-element.10) | copy-start | bytes 3145732
  247.2 3.9 collective-permute-start.11
  264.1 2.8 collective-permute-start.12
  267.0 4.7 %collective-permute-start.13 = (bf16[32,1024]{1,0:T(8,128)(2,1)S(1)}, bf16[32,1024]{1,0:T(8,128)(2,1)S(1)}, u32[]{:S(2)}, u32[]{:S(2)}) collective-permute-start(bf16[32,1024]{1,0:T(8,128)(2,1)S(1)} %maximum_select_fusion.25), channel_id=1, source_target_pairs={{0,16},{8,24},{16,0},{24,8},{32,48},{40,56},{48,32},{56,40},{64,80... | collective-permute-start | bytes 196616 | tf_op jit(solution)/shard_map/ppermute | solution.py:10
  271.7 3.9 collective-permute-start.14
  288.6 32.1 %copy-start.10 = (bf16[4096,128]{1,0:T(8,128)(2,1)S(1)}, bf16[4096,128]{1,0:T(8,128)(2,1)}, u32[]{:S(2)}) copy-start(bf16[4096,128]{1,0:T(8,128)(2,1)} %param.33) | copy-start | bytes 3145732
  288.6 2.8 collective-permute-start.15
  291.4 4.7 %collective-permute-start.16 = (bf16[32,1024]{1,0:T(8,128)(2,1)S(1)}, bf16[32,1024]{1,0:T(8,128)(2,1)S(1)}, u32[]{:S(2)}, u32[]{:S(2)}) collective-permute-start(bf16[32,1024]{1,0:T(8,128)(2,1)S(1)} %maximum_select_fusion.26), channel_id=1, source_target_pairs={{0,16},{8,24},{16,0},{24,8},{32,48},{40,56},{48,32},{56,40},{64,80... | collective-permute-start | bytes 196616 | tf_op jit(solution)/shard_map/ppermute | solution.py:10
  296.2 3.9 collective-permute-start.17
  300.1 39.9 %copy-start.2 = (bf16[4096,256]{0,1:T(8,128)(2,1)S(1)}, bf16[4096,256]{0,1:T(8,128)(2,1)}, u32[]{:S(2)}) copy-start(bf16[4096,256]{0,1:T(8,128)(2,1)} %get-tuple-element.8) | copy-start | bytes 6291460
  312.1 3.1 collective-permute-start.18
  315.3 5.4 %collective-permute-start.19 = (bf16[32,2048]{1,0:T(8,128)(2,1)S(1)}, bf16[32,2048]{1,0:T(8,128)(2,1)S(1)}, u32[]{:S(2)}, u32[]{:S(2)}) collective-permute-start(bf16[32,2048]{1,0:T(8,128)(2,1)S(1)} %maximum_select_fusion.22), channel_id=1, source_target_pairs={{0,16},{8,24},{16,0},{24,8},{32,48},{40,56},{48,32},{56,40},{64,80... | collective-permute-start | bytes 393224 | tf_op jit(solution)/shard_map/ppermute | solution.py:10
  321.0 34.9 %copy-start.3 = (bf16[4096,256]{1,0:T(8,128)(2,1)S(1)}, bf16[4096,256]{1,0:T(8,128)(2,1)}, u32[]{:S(2)}) copy-start(bf16[4096,256]{1,0:T(8,128)(2,1)} %param.32) | copy-start | bytes 6291460
  331.4 3.1 collective-permute-start.20
  334.6 5.4 %collective-permute-start.21 = (bf16[32,2048]{1,0:T(8,128)(2,1)S(1)}, bf16[32,2048]{1,0:T(8,128)(2,1)S(1)}, u32[]{:S(2)}, u32[]{:S(2)}) collective-permute-start(bf16[32,2048]{1,0:T(8,128)(2,1)S(1)} %maximum_select_fusion.23), channel_id=1, source_target_pairs={{0,16},{8,24},{16,0},{24,8},{32,48},{40,56},{48,32},{56,40},{64,80... | collective-permute-start | bytes 393224 | tf_op jit(solution)/shard_map/ppermute | solution.py:10
  340.7 29.4 %copy-start.4 = (bf16[4096,192]{0,1:T(8,128)(2,1)S(1)}, bf16[4096,192]{0,1:T(8,128)(2,1)}, u32[]{:S(2)}) copy-start(bf16[4096,192]{0,1:T(8,128)(2,1)} %get-tuple-element.6) | copy-start | bytes 4718596
  351.6 4.2 %collective-permute-start.22 = (bf16[32,2048]{1,0:T(8,128)(2,1)S(1)}, bf16[32,2048]{1,0:T(8,128)(2,1)S(1)}, u32[]{:S(2)}, u32[]{:S(2)}) collective-permute-start(bf16[32,2048]{1,0:T(8,128)(2,1)S(1)} %bitcast.128), channel_id=1, source_target_pairs={{0,8},{8,0},{16,24},{24,16},{32,40},{40,32},{48,56},{56,48},{64,72... | collective-permute-start | bytes 393224 | tf_op jit(solution)/shard_map/ppermute | solution.py:10
  356.3 29.2 %copy-start.7 = (bf16[1536,192]{0,1:T(8,128)(2,1)S(1)}, bf16[1536,192]{0,1:T(8,128)(2,1)}, u32[]{:S(2)}) copy-start(bf16[1536,192]{0,1:T(8,128)(2,1)} %param.28) | copy-start | bytes 1769476
  365.9 4.2 %collective-permute-start.23 = (bf16[32,2048]{1,0:T(8,128)(2,1)S(1)}, bf16[32,2048]{1,0:T(8,128)(2,1)S(1)}, u32[]{:S(2)}, u32[]{:S(2)}) collective-permute-start(bf16[32,2048]{1,0:T(8,128)(2,1)S(1)} %bitcast.136), channel_id=1, source_target_pairs={{0,8},{8,0},{16,24},{24,16},{32,40},{40,32},{48,56},{56,48},{64,72... | collective-permute-start | bytes 393224 | tf_op jit(solution)/shard_map/ppermute | solution.py:10
Sparse Core Ops, SparseCore 0:
  54.4 24.6 reduce-scatter.3
  117.0 27.3 reduce-scatter.5
  187.9 27.1 reduce-scatter.7
